TPU v7x, 128 devices: a whole 4x4x4 slice. The times are simulated.
128 devices in a mesh: ra: 16 (over x, y_hi, core), dec: 8 (over z, y_lo).
Axes of the slice: x: 4, y: 4 (y_hi: 2, y_lo: 2; y = y_hi * 2 + y_lo), z: 4, core: 2. Of those that a mesh axis runs over, the one named last changes fastest.
Arguments:
- log_flux: float32 [5, 32768], P(None, ('ra', 'dec')), may hold values from 5.5 to 9.5
- position: float32 [2, 32768], P(None, ('ra', 'dec')), may hold values from 0 to 640
- log_width: float32 [32768], P(('ra', 'dec')), may hold values from -3.5 to -0.5
- owner_tile: int32 [32768, 1], P(('ra', 'dec')), may hold values from 0 to 127; in each aligned block of 256 rows (0 to 255, 256 to 511, ...) at most 4 rows name the same one
- sky_level: float32 [16, 8, 5], P('ra', 'dec'), may hold values from 0.5 to 4
- counts: int32 [5, 10240, 5120], P(None, 'ra', 'dec'), may hold values from 0 to 7
Outputs:
- gradient: float32 [8, 32768], P(None, ('ra', 'dec'))
Inputs may be any that keep to these rules, and one draw needn't show every extreme that they name: `owner_tile`: in each aligned block of 256 catalog rows (the rows of one device) no tile is named more than 4 times, a bound that some block reaches.
All inputs are finite; a program needn't handle non-finite values.
Results may differ from a plain program's by a relative error of at most 0.00095.
Values may be sent and summed in bfloat16 or wider, within the bound.
A program may use at most 128 MiB of HBM per device.

v0:
```python
import math
import jax
import jax.numpy as jnp
from jax import lax
from jax.sharding import PartitionSpec as P

MARGIN = 128
CAT_DEV = 256


def passed_along(value, axis, steps):
    count = lax.axis_size(axis)
    leading, last = (max(0, -steps), min(count, count - steps))
    return lax.ppermute(value, axis, [(source, source + steps) for source in range(leading, last)])


def with_halo(cells, sides, width):
    for axis, dim in sides:
        count = lax.axis_size(axis)
        ends = count - 1
        head = lax.slice_in_dim(cells, 0, width, axis=dim)
        tail = lax.slice_in_dim(cells, cells.shape[dim] - width, cells.shape[dim], axis=dim)
        cells = jnp.concatenate(
            [
                lax.ppermute(tail, axis, [(i, (i + 1) % count) for i in range(ends)]),
                cells,
                lax.ppermute(head, axis, [((i + 1) % count, i) for i in range(ends)]),
            ],
            axis=dim,
        )
    return cells


def profiles(center, log_width, length):
    coords = jnp.arange(length, dtype=jnp.float32) - MARGIN + 0.5
    sigma = MARGIN * jnp.exp(log_width)
    offset = (coords[:, None] - center[None, :]) / sigma[None, :]
    shape = jnp.exp(-0.5 * offset * offset) / (math.sqrt(2.0 * math.pi) * sigma[None, :])
    return (shape, offset, sigma)


def on_device(log_flux, position, log_width, owner_tile, sky_level, counts):
    tile_count = lax.axis_size("ra") * lax.axis_size("dec")
    capacity = max(2, 2 * CAT_DEV // tile_count)
    slot_count = tile_count * capacity
    tile_side = counts.shape[1]
    canvas_side = tile_side + 2 * MARGIN
    rows_here = log_flux.shape[1]
    target_tile = owner_tile[:, 0]
    order = jnp.arange(rows_here, dtype=jnp.int32)
    matches = (target_tile[:, None] == target_tile[None, :]) & (order[None, :] < order[:, None])
    rank_in = jnp.sum(matches.astype(jnp.int32), axis=1)
    target_slot = target_tile * capacity + rank_in
    onehot = (target_slot[:, None] == jnp.arange(slot_count, dtype=jnp.int32)[None, :]).astype(
        jnp.float32
    )
    params = jnp.concatenate(
        [log_flux, position, log_width[None, :], jnp.ones((1, rows_here), jnp.float32)], axis=0
    )
    outgoing = jnp.dot(params, onehot, precision=lax.Precision.HIGHEST)
    arrived = lax.all_to_all(outgoing, ("ra", "dec"), split_axis=1, concat_axis=1, tiled=True)
    flux_values = arrived[8][None, :] * jnp.exp(arrived[0:5])
    row_prof, row_off, sigma = profiles(arrived[5], arrived[7], canvas_side)
    col_prof, col_off, _ = profiles(arrived[6], arrived[7], canvas_side)
    row_bf = row_prof.astype(jnp.bfloat16)
    col_bf = col_prof.astype(jnp.bfloat16)
    scaled = (row_prof[None, :, :] * flux_values[:, None, :]).astype(jnp.bfloat16)
    canvas = jnp.einsum("bis,js->bij", scaled, col_bf, preferred_element_type=jnp.float32).astype(
        jnp.bfloat16
    )
    edge = MARGIN
    inner_end = edge + tile_side
    rim_start = tile_side - edge
    interior = canvas[:, edge:inner_end, edge:inner_end].astype(jnp.float32)
    from_below = passed_along(canvas[:, :edge, edge:inner_end], "ra", -1)
    from_above = passed_along(canvas[:, inner_end:, edge:inner_end], "ra", 1)
    from_right = passed_along(canvas[:, edge:inner_end, :edge], "dec", -1)
    from_left = passed_along(canvas[:, edge:inner_end, inner_end:], "dec", 1)
    interior = interior.at[:, rim_start:, :].add(from_below.astype(jnp.float32))
    interior = interior.at[:, :edge, :].add(from_above.astype(jnp.float32))
    interior = interior.at[:, :, rim_start:].add(from_right.astype(jnp.float32))
    interior = interior.at[:, :, :edge].add(from_left.astype(jnp.float32))
    upper_pair = jnp.concatenate([canvas[:, :edge, :edge], canvas[:, :edge, inner_end:]], axis=2)
    lower_pair = jnp.concatenate(
        [canvas[:, inner_end:, :edge], canvas[:, inner_end:, inner_end:]], axis=2
    )
    below_pair = passed_along(upper_pair, "ra", -1)
    above_pair = passed_along(lower_pair, "ra", 1)
    leftward = jnp.concatenate([below_pair[:, :, :edge], above_pair[:, :, :edge]], axis=1)
    rightward = jnp.concatenate([below_pair[:, :, edge:], above_pair[:, :, edge:]], axis=1)
    got_left = passed_along(leftward, "dec", -1).astype(jnp.float32)
    got_right = passed_along(rightward, "dec", 1).astype(jnp.float32)
    interior = interior.at[:, rim_start:, rim_start:].add(got_left[:, :edge])
    interior = interior.at[:, :edge, rim_start:].add(got_left[:, edge:])
    interior = interior.at[:, rim_start:, :edge].add(got_right[:, :edge])
    interior = interior.at[:, :edge, :edge].add(got_right[:, edge:])
    intensity = sky_level.reshape(-1)[:, None, None] + interior
    weights = (counts.astype(jnp.float32) / intensity - 1.0).astype(jnp.bfloat16)
    weight_canvas = with_halo(weights, (("ra", 1), ("dec", 2)), MARGIN)
    along_rows = jnp.einsum(
        "bij,js->bis", weight_canvas, col_bf, preferred_element_type=jnp.float32
    )
    along_cols = jnp.einsum(
        "bij,is->bjs", weight_canvas, row_bf, preferred_element_type=jnp.float32
    )
    flux_grad = flux_values * jnp.sum(row_bf.astype(jnp.float32)[None, :, :] * along_rows, axis=1)
    row_total = jnp.sum(flux_values[:, None, :] * along_rows, axis=0)
    col_total = jnp.sum(flux_values[:, None, :] * along_cols, axis=0)
    row_grad = jnp.sum(row_prof * row_off / sigma[None, :] * row_total, axis=0)
    col_grad = jnp.sum(col_prof * col_off / sigma[None, :] * col_total, axis=0)
    width_grad = jnp.sum(row_prof * (row_off * row_off - 1.0) * row_total, axis=0) + jnp.sum(
        col_prof * (col_off * col_off - 1.0) * col_total, axis=0
    )
    slot_grad = jnp.concatenate(
        [flux_grad, row_grad[None], col_grad[None], width_grad[None]], axis=0
    )
    returned = lax.all_to_all(slot_grad, ("ra", "dec"), split_axis=1, concat_axis=1, tiled=True)
    return jnp.dot(returned, onehot.T, precision=lax.Precision.HIGHEST)


def solution(mesh):
    in_specs = (
        P(None, ("ra", "dec")),
        P(None, ("ra", "dec")),
        P(("ra", "dec")),
        P(("ra", "dec"), None),
        P("ra", "dec", None),
        P(None, "ra", "dec"),
    )
    out_specs = P(None, ("ra", "dec"))
    return jax.shard_map(
        on_device, mesh=mesh, in_specs=in_specs, out_specs=out_specs, check_vma=False
    )
```

profile of v0, /device:TPU:1, one launch (start us, length us, event | category | flops | bytes accessed | tf_op | source)
XLA Modules:
  0.0 254.1 jit_solution(15445283636594914386)
XLA Ops:
  1.7 2.1 fusion.21
  3.8 11.5 %all-to-all-start = ((f32[9,128,4]{0,2,1:T(4,128)}), f32[9,128,4]{0,2,1:T(4,128)S(1)}, u32[]{:S(2)}, u32[]{:S(2)}) async-start(f32[9,128,4]{0,2,1:T(4,128)} %bitcast.4), calls=%async_computation | async-start | bytes 524288 | tf_op jit(solution)/shard_map/all_to_all | solution.py:61
  17.4 10.3 %copy.91 = s32[5,640,640]{1,2,0:T(8,128)} copy(s32[5,640,640]{2,1,0:T(8,128)} %param.27) | data formatting | bytes 16384000 | tf_op args[5]
  30.5 5.1 %convolution_convert_fusion = bf16[5,896,896]{1,2,0:T(8,128)(2,1)S(1)} fusion(f32[5,512]{1,0:T(8,128)S(1)} %broadcast_multiply_fusion, f32[896,512]{1,0:T(8,128)S(1)} %get-tuple-element.132, f32[512]{0:T(512)S(1)} %mul.154, f32[512]{0:T(512)S(1)} %mul.149, f32[512]{0:T(512)S(1)} %sub.53, f32[896]{0:T(1024)S(1)} %iota_add_fusion), kind=kOutput, calls=%fused_computation.6 | convolution fusion | flops 4121772032 | bytes 9883136 | tf_op jit(solution)/shard_map/bis,js->bij/dot_general | solution.py:68
  36.1 5.1 %collective-permute-start.5 = (bf16[5,128,256]{1,2,0:T(8,128)(2,1)S(1)}, bf16[5,128,256]{1,2,0:T(8,128)(2,1)S(1)}, u32[]{:S(2)}, u32[]{:S(2)}) collective-permute-start(bf16[5,128,256]{1,2,0:T(8,128)(2,1)S(1)} %pad_maximum_fusion.5), channel_id=1, source_target_pairs={{0,8},{8,16},{16,24},{24,32},{32,40},{40,48},{48,56},{56,64},{64,7... | collective-permute-start | bytes 983048 | tf_op jit(solution)/shard_map/ppermute | solution.py:14
  41.2 1.9 collective-permute-start.4
  43.3 5.1 %collective-permute-start.1 = (bf16[5,128,640]{1,2,0:T(8,128)(2,1)S(1)}, bf16[5,128,640]{1,2,0:T(8,128)(2,1)S(1)}, u32[]{:S(2)}, u32[]{:S(2)}) collective-permute-start(bf16[5,128,640]{1,2,0:T(8,128)(2,1)S(1)} %get-tuple-element.120), channel_id=1, source_target_pairs={{0,8},{8,16},{16,24},{24,32},{32,40},{40,48},{48,56},{56,64},{64,7... | collective-permute-start | bytes 2457608 | tf_op jit(solution)/shard_map/ppermute | solution.py:14
  53.2 4.6 %collective-permute-start.7 = (bf16[5,256,128]{1,2,0:T(8,128)(2,1)S(1)}, bf16[5,256,128]{1,2,0:T(8,128)(2,1)S(1)}, u32[]{:S(2)}, u32[]{:S(2)}) collective-permute-start(bf16[5,256,128]{1,2,0:T(8,128)(2,1)S(1)} %pad_maximum_fusion.7), channel_id=1, source_target_pairs={{0,1},{1,2},{2,3},{3,4},{4,5},{5,6},{6,7},{8,9},{9,10},{10,11},{11... | collective-permute-start | bytes 983048 | tf_op jit(solution)/shard_map/ppermute | solution.py:14
  58.4 43.4 %collective-permute-done.6 = bf16[5,256,128]{1,2,0:T(8,128)(2,1)S(1)} collective-permute-done((bf16[5,256,128]{1,2,0:T(8,128)(2,1)S(1)}, bf16[5,256,128]{1,2,0:T(8,128)(2,1)S(1)}, u32[]{:S(2)}, u32[]{:S(2)}) %collective-permute-start.6) | collective-permute-done | bytes 327712 | tf_op jit(solution)/shard_map/ppermute | solution.py:14
  101.8 3.6 %collective-permute-start.3 = (bf16[5,640,128]{1,2,0:T(8,128)(2,1)S(1)}, bf16[5,640,128]{1,2,0:T(8,128)(2,1)S(1)}, u32[]{:S(2)}, u32[]{:S(2)}) collective-permute-start(bf16[5,640,128]{1,2,0:T(8,128)(2,1)S(1)} %get-tuple-element.118), channel_id=1, source_target_pairs={{0,1},{1,2},{2,3},{3,4},{4,5},{5,6},{6,7},{8,9},{9,10},{10,11},{11... | collective-permute-start | bytes 2457608 | tf_op jit(solution)/shard_map/ppermute | solution.py:14
  106.6 7.9 %collective-permute-done.3 = bf16[5,640,128]{1,2,0:T(8,128)(2,1)S(1)} collective-permute-done((bf16[5,640,128]{1,2,0:T(8,128)(2,1)S(1)}, bf16[5,640,128]{1,2,0:T(8,128)(2,1)S(1)}, u32[]{:S(2)}, u32[]{:S(2)}) %collective-permute-start.3) | collective-permute-done | bytes 819232 | tf_op jit(solution)/shard_map/ppermute | solution.py:14
  114.9 3.2 %copy-done = f32[5,640,640]{1,2,0:T(8,128)} copy-done((f32[5,640,640]{1,2,0:T(8,128)}, f32[5,640,640]{1,2,0:T(8,128)S(1)}, u32[]{:S(2)}) %copy-start) | copy-done | bytes 8192024
  118.1 2.1 add_select_fusion
  120.2 5.8 %scatter-add.35 = f32[5,640,640]{1,2,0:T(8,128)} dynamic-update-slice(f32[5,640,640]{1,2,0:T(8,128)} %copy-done, f32[5,128,128]{1,2,0:T(8,128)S(1)} %add_select_fusion, s32[]{:T(128)} %constant.235.clone.1, s32[]{:T(128)} %bitcast.8, s32[]{:T(128)} %bitcast.9) | dynamic-update-slice | bytes 655364 | tf_op jit(solution)/shard_map/scatter-add | solution.py:94
  129.5 7.3 %add_convert_fusion = bf16[5,640,640]{1,2,0:T(8,128)(2,1)S(1)} fusion(f32[5,640,640]{1,2,0:T(8,128)} %fusion.22, s32[5,640,640]{1,2,0:T(8,128)} %copy.91, f32[5]{0:T(128)S(1)} %bitcast.31), kind=kLoop, calls=%fused_computation.4 | loop fusion | flops 10240000 | bytes 20480020 | tf_op jit(solution)/shard_map/convert_element_type | solution.py:98
  139.1 2.5 collective-permute-start.9
  141.5 20.7 %collective-permute-done.8 = bf16[5,128,640]{1,2,0:T(8,128)(2,1)S(1)} collective-permute-done((bf16[5,128,640]{1,2,0:T(8,128)(2,1)S(1)}, bf16[5,128,640]{1,2,0:T(8,128)(2,1)S(1)}, u32[]{:S(2)}, u32[]{:S(2)}) %collective-permute-start.8) | collective-permute-done | bytes 819232 | tf_op jit(solution)/shard_map/ppermute | solution.py:25
  164.2 6.1 %collective-permute-start.10 = (bf16[5,896,128]{1,2,0:T(8,128)(2,1)}, bf16[5,896,128]{1,2,0:T(8,128)(2,1)}, u32[]{:S(2)}, u32[]{:S(2)}) collective-permute-start(bf16[5,896,128]{1,2,0:T(8,128)(2,1)} %get-tuple-element.122), channel_id=1, source_target_pairs={{0,1},{1,2},{2,3},{3,4},{4,5},{5,6},{6,7},{8,9},{9,10},{10,11},{11... | collective-permute-start | bytes 3440648 | tf_op jit(solution)/shard_map/ppermute | solution.py:25
  171.7 10.6 %collective-permute-done.10 = bf16[5,896,128]{1,2,0:T(8,128)(2,1)} collective-permute-done((bf16[5,896,128]{1,2,0:T(8,128)(2,1)}, bf16[5,896,128]{1,2,0:T(8,128)(2,1)}, u32[]{:S(2)}, u32[]{:S(2)}) %collective-permute-start.10) | collective-permute-done | bytes 1146912 | tf_op jit(solution)/shard_map/ppermute | solution.py:25
  182.3 27.7 %collective-permute-done.11 = bf16[5,896,128]{1,2,0:T(8,128)(2,1)} collective-permute-done((bf16[5,896,128]{1,2,0:T(8,128)(2,1)}, bf16[5,896,128]{1,2,0:T(8,128)(2,1)}, u32[]{:S(2)}, u32[]{:S(2)}) %collective-permute-start.11) | collective-permute-done | bytes 1146912 | tf_op jit(solution)/shard_map/ppermute | solution.py:27
  210.0 9.9 %multiply_reduce_fusion = f32[896,512]{1,0:T(8,128)S(1)} fusion(f32[5,512]{1,0:T(8,128)S(1)} %broadcast_multiply_fusion, f32[512]{0:T(512)S(1)} %mul.154, f32[512]{0:T(512)S(1)} %mul.149, f32[512]{0:T(512)S(1)} %sub.50, f32[896]{0:T(1024)S(1)} %iota_add_fusion, bf16[5,896,128]{1,2,0:T(8,128)(2,1)} %collective-permute-done.11, ...), kind=kOutput, calls=%fused_computation | convolution fusion | flops 4157440000 | bytes 9883136 | tf_op jit(solution)/shard_map/bij,is->bjs/dot_general | solution.py:103
  220.0 7.7 %multiply_reduce_fusion.2 = (f32[5,512]{1,0:T(8,128)S(1)}, f32[896,512]{1,0:T(8,128)S(1)}) fusion(f32[896,512]{1,0:T(8,128)S(1)} %get-tuple-element.131, f32[5,512]{1,0:T(8,128)S(1)} %broadcast_multiply_fusion, f32[512]{0:T(512)S(1)} %mul.154, f32[512]{0:T(512)S(1)} %mul.149, f32[512]{0:T(512)S(1)} %sub.53, f32[896]{0:T(1024)S(1)} %iota_add_fusion, ...), kind=kOutput, calls=%fused_computation.2 | convolution fusion | flops 4162024960 | bytes 11728384 | tf_op jit(solution)/shard_map/bij,js->bis/dot_general | solution.py:100
  227.7 2.2 multiply_reduce_fusion.6
  231.2 21.9 %all_to_all.18 = f32[8,128,4]{0,2,1:T(4,128)S(1)} all-to-all(f32[8,128,4]{0,2,1:T(4,128)S(1)} %copy.98), channel_id=1, replica_groups=mesh['ra'=16,'dec'=8] {'ra','dec'}, dimensions={1} | all-to-all | bytes 32768 | tf_op jit(solution)/shard_map/all_to_all | solution.py:117
  (82 shorter events, 25.2 us)
Async XLA Ops:
  3.8 23.8 %all-to-all-start = ((f32[9,128,4]{0,2,1:T(4,128)}), f32[9,128,4]{0,2,1:T(4,128)S(1)}, u32[]{:S(2)}, u32[]{:S(2)}) async-start(f32[9,128,4]{0,2,1:T(4,128)} %bitcast.4), calls=%async_computation | async-start | bytes 524288 | tf_op jit(solution)/shard_map/all_to_all | solution.py:61
  36.1 15.6 %collective-permute-start.5 = (bf16[5,128,256]{1,2,0:T(8,128)(2,1)S(1)}, bf16[5,128,256]{1,2,0:T(8,128)(2,1)S(1)}, u32[]{:S(2)}, u32[]{:S(2)}) collective-permute-start(bf16[5,128,256]{1,2,0:T(8,128)(2,1)S(1)} %pad_maximum_fusion.5), channel_id=1, source_target_pairs={{0,8},{8,16},{16,24},{24,32},{32,40},{40,48},{48,56},{56,64},{64,7... | collective-permute-start | bytes 983048 | tf_op jit(solution)/shard_map/ppermute | solution.py:14
  41.2 10.5 %collective-permute-start.4 = (bf16[5,128,256]{1,2,0:T(8,128)(2,1)S(1)}, bf16[5,128,256]{1,2,0:T(8,128)(2,1)S(1)}, u32[]{:S(2)}, u32[]{:S(2)}) collective-permute-start(bf16[5,128,256]{1,2,0:T(8,128)(2,1)S(1)} %pad_maximum_fusion.4), channel_id=1, source_target_pairs={{8,0},{16,8},{24,16},{32,24},{40,32},{48,40},{56,48},{64,56},{72,6... | collective-permute-start | bytes 983048 | tf_op jit(solution)/shard_map/ppermute | solution.py:14
  43.3 62.5 %collective-permute-start.1 = (bf16[5,128,640]{1,2,0:T(8,128)(2,1)S(1)}, bf16[5,128,640]{1,2,0:T(8,128)(2,1)S(1)}, u32[]{:S(2)}, u32[]{:S(2)}) collective-permute-start(bf16[5,128,640]{1,2,0:T(8,128)(2,1)S(1)} %get-tuple-element.120), channel_id=1, source_target_pairs={{0,8},{8,16},{16,24},{24,32},{32,40},{40,48},{48,56},{56,64},{64,7... | collective-permute-start | bytes 2457608 | tf_op jit(solution)/shard_map/ppermute | solution.py:14
  48.5 57.0 %collective-permute-start = (bf16[5,128,640]{1,2,0:T(8,128)(2,1)S(1)}, bf16[5,128,640]{1,2,0:T(8,128)(2,1)S(1)}, u32[]{:S(2)}, u32[]{:S(2)}) collective-permute-start(bf16[5,128,640]{1,2,0:T(8,128)(2,1)S(1)} %get-tuple-element.121), channel_id=1, source_target_pairs={{8,0},{16,8},{24,16},{32,24},{40,32},{48,40},{56,48},{64,56},{72,6... | collective-permute-start | bytes 2457608 | tf_op jit(solution)/shard_map/ppermute | solution.py:14
  50.4 55.8 %collective-permute-start.2 = (bf16[5,640,128]{1,2,0:T(8,128)(2,1)S(1)}, bf16[5,640,128]{1,2,0:T(8,128)(2,1)S(1)}, u32[]{:S(2)}, u32[]{:S(2)}) collective-permute-start(bf16[5,640,128]{1,2,0:T(8,128)(2,1)S(1)} %get-tuple-element.119), channel_id=1, source_target_pairs={{1,0},{2,1},{3,2},{4,3},{5,4},{6,5},{7,6},{9,8},{10,9},{11,10},{12... | collective-permute-start | bytes 2457608 | tf_op jit(solution)/shard_map/ppermute | solution.py:14
  51.9 50.0 %collective-permute-start.6 = (bf16[5,256,128]{1,2,0:T(8,128)(2,1)S(1)}, bf16[5,256,128]{1,2,0:T(8,128)(2,1)S(1)}, u32[]{:S(2)}, u32[]{:S(2)}) collective-permute-start(bf16[5,256,128]{1,2,0:T(8,128)(2,1)S(1)} %pad_maximum_fusion.6), channel_id=1, source_target_pairs={{1,0},{2,1},{3,2},{4,3},{5,4},{6,5},{7,6},{9,8},{10,9},{11,10},{12... | collective-permute-start | bytes 983048 | tf_op jit(solution)/shard_map/ppermute | solution.py:14
  53.2 52.3 %collective-permute-start.7 = (bf16[5,256,128]{1,2,0:T(8,128)(2,1)S(1)}, bf16[5,256,128]{1,2,0:T(8,128)(2,1)S(1)}, u32[]{:S(2)}, u32[]{:S(2)}) collective-permute-start(bf16[5,256,128]{1,2,0:T(8,128)(2,1)S(1)} %pad_maximum_fusion.7), channel_id=1, source_target_pairs={{0,1},{1,2},{2,3},{3,4},{4,5},{5,6},{6,7},{8,9},{9,10},{10,11},{11... | collective-permute-start | bytes 983048 | tf_op jit(solution)/shard_map/ppermute | solution.py:14
  101.8 12.6 %collective-permute-start.3 = (bf16[5,640,128]{1,2,0:T(8,128)(2,1)S(1)}, bf16[5,640,128]{1,2,0:T(8,128)(2,1)S(1)}, u32[]{:S(2)}, u32[]{:S(2)}) collective-permute-start(bf16[5,640,128]{1,2,0:T(8,128)(2,1)S(1)} %get-tuple-element.118), channel_id=1, source_target_pairs={{0,1},{1,2},{2,3},{3,4},{4,5},{5,6},{6,7},{8,9},{9,10},{10,11},{11... | collective-permute-start | bytes 2457608 | tf_op jit(solution)/shard_map/ppermute | solution.py:14
  114.9 3.2 %copy-start = (f32[5,640,640]{1,2,0:T(8,128)}, f32[5,640,640]{1,2,0:T(8,128)S(1)}, u32[]{:S(2)}) copy-start(f32[5,640,640]{1,2,0:T(8,128)S(1)} %fusion.24) | copy-start | bytes 24576004
  114.9 14.7 %copy-start.7 = (f32[1,1,5]{2,1,0:T(1,128)S(1)}, f32[1,1,5]{2,1,0:T(1,128)}, u32[]{:S(2)}) copy-start(f32[1,1,5]{2,1,0:T(1,128)} %param.26) | copy-start | bytes 64
  136.8 27.3 %copy-start.1 = (bf16[5,640,640]{1,2,0:T(8,128)(2,1)}, bf16[5,640,640]{1,2,0:T(8,128)(2,1)S(1)}, u32[]{:S(2)}) copy-start(bf16[5,640,640]{1,2,0:T(8,128)(2,1)S(1)} %add_convert_fusion) | copy-start | bytes 12288004
  137.1 25.1 %collective-permute-start.8 = (bf16[5,128,640]{1,2,0:T(8,128)(2,1)S(1)}, bf16[5,128,640]{1,2,0:T(8,128)(2,1)S(1)}, u32[]{:S(2)}, u32[]{:S(2)}) collective-permute-start(bf16[5,128,640]{1,2,0:T(8,128)(2,1)S(1)} %get-tuple-element.124), channel_id=1, source_target_pairs={{0,8},{8,16},{16,24},{24,32},{32,40},{40,48},{48,56},{56,64},{64,7... | collective-permute-start | bytes 2457608 | tf_op jit(solution)/shard_map/ppermute | solution.py:25
  139.1 23.2 %collective-permute-start.9 = (bf16[5,128,640]{1,2,0:T(8,128)(2,1)S(1)}, bf16[5,128,640]{1,2,0:T(8,128)(2,1)S(1)}, u32[]{:S(2)}, u32[]{:S(2)}) collective-permute-start(bf16[5,128,640]{1,2,0:T(8,128)(2,1)S(1)} %get-tuple-element.125), channel_id=1, source_target_pairs={{8,0},{16,8},{24,16},{32,24},{40,32},{48,40},{56,48},{64,56},{72,6... | collective-permute-start | bytes 2457608 | tf_op jit(solution)/shard_map/ppermute | solution.py:27
  162.2 1.9 copy-start.3
  162.2 1.9 copy-start.5
  164.2 18.2 %collective-permute-start.10 = (bf16[5,896,128]{1,2,0:T(8,128)(2,1)}, bf16[5,896,128]{1,2,0:T(8,128)(2,1)}, u32[]{:S(2)}, u32[]{:S(2)}) collective-permute-start(bf16[5,896,128]{1,2,0:T(8,128)(2,1)} %get-tuple-element.122), channel_id=1, source_target_pairs={{0,1},{1,2},{2,3},{3,4},{4,5},{5,6},{6,7},{8,9},{9,10},{10,11},{11... | collective-permute-start | bytes 3440648 | tf_op jit(solution)/shard_map/ppermute | solution.py:25
  170.3 39.8 %collective-permute-start.11 = (bf16[5,896,128]{1,2,0:T(8,128)(2,1)}, bf16[5,896,128]{1,2,0:T(8,128)(2,1)}, u32[]{:S(2)}, u32[]{:S(2)}) collective-permute-start(bf16[5,896,128]{1,2,0:T(8,128)(2,1)} %get-tuple-element.123), channel_id=1, source_target_pairs={{1,0},{2,1},{3,2},{4,3},{5,4},{6,5},{7,6},{9,8},{10,9},{11,10},{12... | collective-permute-start | bytes 3440648 | tf_op jit(solution)/shard_map/ppermute | solution.py:27
  171.7 48.3 %copy-start.2 = (bf16[5,640,640]{1,2,0:T(8,128)(2,1)S(1)}, bf16[5,640,640]{1,2,0:T(8,128)(2,1)}, u32[]{:S(2)}) copy-start(bf16[5,640,640]{1,2,0:T(8,128)(2,1)} %copy-done.1) | copy-start | bytes 12288004
  171.7 48.3 %copy-start.4 = (bf16[5,128,640]{1,2,0:T(8,128)(2,1)S(1)}, bf16[5,128,640]{1,2,0:T(8,128)(2,1)}, u32[]{:S(2)}) copy-start(bf16[5,128,640]{1,2,0:T(8,128)(2,1)} %copy-done.3) | copy-start | bytes 2457604
  171.7 48.3 %copy-start.6 = (bf16[5,128,640]{1,2,0:T(8,128)(2,1)S(1)}, bf16[5,128,640]{1,2,0:T(8,128)(2,1)}, u32[]{:S(2)}) copy-start(bf16[5,128,640]{1,2,0:T(8,128)(2,1)} %copy-done.5) | copy-start | bytes 2457604
where the time goes:
time: 255 us; the launch traced here: 254 us
  waiting for transfers between devices  110 us (43%)
  starting transfers between devices  48.1 us (19%)
  matrix products  25.9 us (10%)
  other arithmetic  24.2 us (9%)
  local copies, waits for them, and re-layouts  23.2 us (9%)
  blocking collectives  21.9 us (9%)
    ppermute x8, waiting for transfers between devices, passed_along(): lax.ppermute(value, axis, [(source, source + steps) for source in range(l...  51.3 us
    ppermute x2, waiting for transfers between devices, with_halo(): lax.ppermute(tail, axis, [(i, (i + 1) % count) for i in range(ends)])  31.4 us
    ppermute x2, waiting for transfers between devices, with_halo(): lax.ppermute(head, axis, [((i + 1) % count, i) for i in range(ends)])  27.7 us
    ppermute x8, starting transfers between devices, passed_along(): lax.ppermute(value, axis, [(source, source + steps) for source in range(l...  24.8 us
    all_to_all x1, blocking collectives, on_device(): lax.all_to_all(slot_grad, ('ra', 'dec'), split_axis=1, concat_axis=1, til...  21.9 us
    unnamed x18, local copies, waits for them, and re-layouts  13.6 us
    all_to_all x1, starting transfers between devices, on_device(): lax.all_to_all(outgoing, ('ra', 'dec'), split_axis=1, concat_axis=1, tile...  11.5 us
    dot_general x1, matrix products, on_device(): jnp.einsum('bij,is->bjs', weight_canvas, row_bf, preferred_element_type=j...  9.9 us
  transfers between devices with their start and end apart: 13, of which 5 were waited for; matrix products, arithmetic and copies ran while one was open for 6% of the time, Pallas kernels for 0%

commit v1 on v0

--- a/solution.py
+++ b/solution.py
@@ -58,7 +58,15 @@
         [log_flux, position, log_width[None, :], jnp.ones((1, rows_here), jnp.float32)], axis=0
     )
     outgoing = jnp.dot(params, onehot, precision=lax.Precision.HIGHEST)
-    arrived = lax.all_to_all(outgoing, ("ra", "dec"), split_axis=1, concat_axis=1, tiled=True)
+    arrived = jnp.concatenate(
+        lax.all_to_all(
+            jnp.stack(jnp.split(outgoing, lax.axis_size(("ra", "dec")), axis=1)),
+            ("ra", "dec"),
+            0,
+            0,
+        ),
+        axis=1,
+    )
     flux_values = arrived[8][None, :] * jnp.exp(arrived[0:5])
     row_prof, row_off, sigma = profiles(arrived[5], arrived[7], canvas_side)
     col_prof, col_off, _ = profiles(arrived[6], arrived[7], canvas_side)

time: 255 us -> 334 us (1.31)
  local copies, waits for them, and re-layouts: 23.2 us -> 110 us
  matrix products: 25.9 us -> 20.1 us
  waiting for transfers between devices: 110 us -> 115 us
    unnamed x18 -> x138, local copies, waits for them, and re-layouts: 13.6 us -> 86.9 us
    split x0 -> x135, local copies, waits for them, and re-layouts: none -> 12.3 us  [on_device(): jnp.split(outgoing, lax.axis_size(('ra', 'dec')), axis=1)]
    dot_general x1, matrix products: 9.9 us -> 5.23 us  [on_device(): jnp.einsum('bij,is->bjs', weight_canvas, row_bf, preferred_element_type=j...]
    ppermute x2, waiting for transfers between devices: 31.4 us -> 35 us  [with_halo(): lax.ppermute(tail, axis, [(i, (i + 1) % count) for i in range(ends)])]
  transfers between devices with their start and end apart: 13 -> 13, of which waited for: 5 -> 5; matrix products, arithmetic and copies ran while one was open for 6% -> 4% of each run, Pallas kernels for 0% -> 0%
where the time goes in v1:
time: 334 us; the launch traced here: 333 us
  waiting for transfers between devices  115 us (34%)
  local copies, waits for them, and re-layouts  110 us (33%)
  starting transfers between devices  45.5 us (14%)
  blocking collectives  21.1 us (6%)
  other arithmetic  20.9 us (6%)
  matrix products  20.1 us (6%)
    unnamed x138, local copies, waits for them, and re-layouts  86.9 us
    ppermute x8, waiting for transfers between devices, passed_along(): lax.ppermute(value, axis, [(source, source + steps) for source in range(l...  51.3 us
    ppermute x2, waiting for transfers between devices, with_halo(): lax.ppermute(tail, axis, [(i, (i + 1) % count) for i in range(ends)])  35 us
    ppermute x2, waiting for transfers between devices, with_halo(): lax.ppermute(head, axis, [((i + 1) % count, i) for i in range(ends)])  28.3 us
    ppermute x8, starting transfers between devices, passed_along(): lax.ppermute(value, axis, [(source, source + steps) for source in range(l...  24.8 us
    all_to_all x1, blocking collectives, on_device(): lax.all_to_all(slot_grad, ('ra', 'dec'), split_axis=1, concat_axis=1, til...  21.1 us
    split x135, local copies, waits for them, and re-layouts, on_device(): jnp.split(outgoing, lax.axis_size(('ra', 'dec')), axis=1)  12.3 us
    all_to_all x1, starting transfers between devices, on_device(): lax.all_to_all(jnp.stack(jnp.split(outgoing, lax.axis_size(('ra', 'dec'))...  11.5 us
  transfers between devices with their start and end apart: 13, of which 5 were waited for; matrix products, arithmetic and copies ran while one was open for 4% of the time, Pallas kernels for 0%

profile of v1, /device:TPU:1, one launch (start us, length us, event | category | flops | bytes accessed | tf_op | source)
XLA Modules:
  0.0 333.5 jit_solution(16713871122803871856)
XLA Ops:
  89.3 11.5 %all-to-all-start = ((f32[128,9,4]{1,2,0:T(4,128)}), f32[128,9,4]{1,2,0:T(4,128)S(1)}, u32[]{:S(2)}, u32[]{:S(2)}) async-start(f32[128,9,4]{1,2,0:T(4,128)} %constant_dynamic-update-slice_fusion), calls=%async_computation | async-start | bytes 524288 | tf_op jit(solution)/shard_map/all_to_all | solution.py:62
  102.1 10.3 %copy.1206 = s32[5,640,640]{1,2,0:T(8,128)} copy(s32[5,640,640]{2,1,0:T(8,128)} %param.27) | data formatting | bytes 16384000 | tf_op args[5]
  114.7 5.1 %convolution_convert_fusion = bf16[5,896,896]{1,2,0:T(8,128)(2,1)S(1)} fusion(f32[5,512]{1,0:T(8,128)S(1)} %broadcast_multiply_fusion, f32[896,512]{1,0:T(8,128)S(1)} %get-tuple-element.260, f32[512]{0:T(512)S(1)} %mul.158, f32[512]{0:T(512)S(1)} %mul.153, f32[512]{0:T(512)S(1)} %sub.53, f32[896]{0:T(1024)S(1)} %iota_add_fusion), kind=kOutput, calls=%fused_computation.6 | convolution fusion | flops 4121772032 | bytes 9883136 | tf_op jit(solution)/shard_map/bis,js->bij/dot_general | solution.py:76
  120.4 5.1 %collective-permute-start.5 = (bf16[5,128,256]{1,2,0:T(8,128)(2,1)S(1)}, bf16[5,128,256]{1,2,0:T(8,128)(2,1)S(1)}, u32[]{:S(2)}, u32[]{:S(2)}) collective-permute-start(bf16[5,128,256]{1,2,0:T(8,128)(2,1)S(1)} %pad_maximum_fusion.6), channel_id=1, source_target_pairs={{0,8},{8,16},{16,24},{24,32},{32,40},{40,48},{48,56},{56,64},{64,7... | collective-permute-start | bytes 983048 | tf_op jit(solution)/shard_map/ppermute | solution.py:14
  125.5 1.9 collective-permute-start.4
  127.6 5.1 %collective-permute-start.1 = (bf16[5,128,640]{1,2,0:T(8,128)(2,1)S(1)}, bf16[5,128,640]{1,2,0:T(8,128)(2,1)S(1)}, u32[]{:S(2)}, u32[]{:S(2)}) collective-permute-start(bf16[5,128,640]{1,2,0:T(8,128)(2,1)S(1)} %get-tuple-element.115), channel_id=1, source_target_pairs={{0,8},{8,16},{16,24},{24,32},{32,40},{40,48},{48,56},{56,64},{64,7... | collective-permute-start | bytes 2457608 | tf_op jit(solution)/shard_map/ppermute | solution.py:14
  132.7 1.9 collective-permute-start
  137.4 4.6 %collective-permute-start.7 = (bf16[5,256,128]{1,2,0:T(8,128)(2,1)S(1)}, bf16[5,256,128]{1,2,0:T(8,128)(2,1)S(1)}, u32[]{:S(2)}, u32[]{:S(2)}) collective-permute-start(bf16[5,256,128]{1,2,0:T(8,128)(2,1)S(1)} %pad_maximum_fusion.8), channel_id=1, source_target_pairs={{0,1},{1,2},{2,3},{3,4},{4,5},{5,6},{6,7},{8,9},{9,10},{10,11},{11... | collective-permute-start | bytes 983048 | tf_op jit(solution)/shard_map/ppermute | solution.py:14
  142.6 43.4 %collective-permute-done.6 = bf16[5,256,128]{1,2,0:T(8,128)(2,1)S(1)} collective-permute-done((bf16[5,256,128]{1,2,0:T(8,128)(2,1)S(1)}, bf16[5,256,128]{1,2,0:T(8,128)(2,1)S(1)}, u32[]{:S(2)}, u32[]{:S(2)}) %collective-permute-start.6) | collective-permute-done | bytes 327712 | tf_op jit(solution)/shard_map/ppermute | solution.py:14
  186.0 3.6 %collective-permute-start.3 = (bf16[5,640,128]{1,2,0:T(8,128)(2,1)S(1)}, bf16[5,640,128]{1,2,0:T(8,128)(2,1)S(1)}, u32[]{:S(2)}, u32[]{:S(2)}) collective-permute-start(bf16[5,640,128]{1,2,0:T(8,128)(2,1)S(1)} %get-tuple-element.113), channel_id=1, source_target_pairs={{0,1},{1,2},{2,3},{3,4},{4,5},{5,6},{6,7},{8,9},{9,10},{10,11},{11... | collective-permute-start | bytes 2457608 | tf_op jit(solution)/shard_map/ppermute | solution.py:14
  190.8 7.9 %collective-permute-done.3 = bf16[5,640,128]{1,2,0:T(8,128)(2,1)S(1)} collective-permute-done((bf16[5,640,128]{1,2,0:T(8,128)(2,1)S(1)}, bf16[5,640,128]{1,2,0:T(8,128)(2,1)S(1)}, u32[]{:S(2)}, u32[]{:S(2)}) %collective-permute-start.3) | collective-permute-done | bytes 819232 | tf_op jit(solution)/shard_map/ppermute | solution.py:14
  199.1 3.1 copy-done
  202.3 2.1 add_select_fusion
  204.4 5.8 %scatter-add.35 = f32[5,640,640]{1,2,0:T(8,128)} dynamic-update-slice(f32[5,640,640]{1,2,0:T(8,128)} %copy-done, f32[5,128,128]{1,2,0:T(8,128)S(1)} %add_select_fusion, s32[]{:T(128)} %constant.235.clone.1, s32[]{:T(128)} %bitcast.136, s32[]{:T(128)} %bitcast.137) | dynamic-update-slice | bytes 655364 | tf_op jit(solution)/shard_map/scatter-add | solution.py:102
  213.8 7.3 %add_convert_fusion = bf16[5,640,640]{1,2,0:T(8,128)(2,1)S(1)} fusion(f32[5,640,640]{1,2,0:T(8,128)} %fusion.22, s32[5,640,640]{1,2,0:T(8,128)} %copy.1206, f32[5]{0:T(128)S(1)} %bitcast.287), kind=kLoop, calls=%fused_computation.4 | loop fusion | flops 10240000 | bytes 20480020 | tf_op jit(solution)/shard_map/convert_element_type | solution.py:106
  223.4 2.5 collective-permute-start.9
  225.8 22.4 %collective-permute-done.8 = bf16[5,128,640]{1,2,0:T(8,128)(2,1)S(1)} collective-permute-done((bf16[5,128,640]{1,2,0:T(8,128)(2,1)S(1)}, bf16[5,128,640]{1,2,0:T(8,128)(2,1)S(1)}, u32[]{:S(2)}, u32[]{:S(2)}) %collective-permute-start.8) | collective-permute-done | bytes 819232 | tf_op jit(solution)/shard_map/ppermute | solution.py:25
  248.5 3.5 %collective-permute-start.10 = (bf16[5,896,128]{1,2,0:T(8,128)(2,1)S(1)}, bf16[5,896,128]{1,2,0:T(8,128)(2,1)S(1)}, u32[]{:S(2)}, u32[]{:S(2)}) collective-permute-start(bf16[5,896,128]{1,2,0:T(8,128)(2,1)S(1)} %get-tuple-element.117), channel_id=1, source_target_pairs={{0,1},{1,2},{2,3},{3,4},{4,5},{5,6},{6,7},{8,9},{9,10},{10,11},{11... | collective-permute-start | bytes 3440648 | tf_op jit(solution)/shard_map/ppermute | solution.py:25
  253.3 12.7 %collective-permute-done.10 = bf16[5,896,128]{1,2,0:T(8,128)(2,1)S(1)} collective-permute-done((bf16[5,896,128]{1,2,0:T(8,128)(2,1)S(1)}, bf16[5,896,128]{1,2,0:T(8,128)(2,1)S(1)}, u32[]{:S(2)}, u32[]{:S(2)}) %collective-permute-start.10) | collective-permute-done | bytes 1146912 | tf_op jit(solution)/shard_map/ppermute | solution.py:25
  266.0 28.3 %collective-permute-done.11 = bf16[5,896,128]{1,2,0:T(8,128)(2,1)S(1)} collective-permute-done((bf16[5,896,128]{1,2,0:T(8,128)(2,1)S(1)}, bf16[5,896,128]{1,2,0:T(8,128)(2,1)S(1)}, u32[]{:S(2)}, u32[]{:S(2)}) %collective-permute-start.11) | collective-permute-done | bytes 1146912 | tf_op jit(solution)/shard_map/ppermute | solution.py:27
  294.3 5.2 %multiply_reduce_fusion = f32[896,512]{1,0:T(8,128)S(1)} fusion(f32[5,512]{1,0:T(8,128)S(1)} %broadcast_multiply_fusion, f32[512]{0:T(512)S(1)} %mul.158, f32[512]{0:T(512)S(1)} %mul.153, f32[512]{0:T(512)S(1)} %sub.50, f32[896]{0:T(1024)S(1)} %iota_add_fusion, bf16[5,896,128]{1,2,0:T(8,128)(2,1)S(1)} %collective-permute-done.11, ...), kind=kOutput, calls=%fused_computation | convolution fusion | flops 4157440000 | bytes 9883136 | tf_op jit(solution)/shard_map/bij,is->bjs/dot_general | solution.py:111
  299.5 7.7 %multiply_reduce_fusion.2 = (f32[5,512]{1,0:T(8,128)S(1)}, f32[896,512]{1,0:T(8,128)S(1)}) fusion(f32[896,512]{1,0:T(8,128)S(1)} %get-tuple-element.259, f32[5,512]{1,0:T(8,128)S(1)} %broadcast_multiply_fusion, f32[512]{0:T(512)S(1)} %mul.158, f32[512]{0:T(512)S(1)} %mul.153, f32[512]{0:T(512)S(1)} %sub.53, f32[896]{0:T(1024)S(1)} %iota_add_fusion, ...), kind=kOutput, calls=%fused_computation.2 | convolution fusion | flops 4162024960 | bytes 11728384 | tf_op jit(solution)/shard_map/bij,js->bis/dot_general | solution.py:108
  307.2 2.5 multiply_reduce_fusion.6
  311.4 21.1 %all_to_all.14 = f32[8,128,4]{0,2,1:T(4,128)S(1)} all-to-all(f32[8,128,4]{0,2,1:T(4,128)S(1)} %copy.1208), channel_id=1, replica_groups=mesh['ra'=16,'dec'=8] {'ra','dec'}, dimensions={1} | all-to-all | bytes 32768 | tf_op jit(solution)/shard_map/all_to_all | solution.py:125
  (333 shorter events, 108.3 us)
Async XLA Ops:
  3.2 98.2 %copy-start.2 = (s32[3]{0:T(128)S(1)}, s32[3]{0:T(128)}, u32[]{:S(2)}) copy-start(s32[3]{0:T(128)} %constant.242.clone.1) | copy-start | bytes 40
  89.3 23.1 %all-to-all-start = ((f32[128,9,4]{1,2,0:T(4,128)}), f32[128,9,4]{1,2,0:T(4,128)S(1)}, u32[]{:S(2)}, u32[]{:S(2)}) async-start(f32[128,9,4]{1,2,0:T(4,128)} %constant_dynamic-update-slice_fusion), calls=%async_computation | async-start | bytes 524288 | tf_op jit(solution)/shard_map/all_to_all | solution.py:62
  120.4 15.6 %collective-permute-start.5 = (bf16[5,128,256]{1,2,0:T(8,128)(2,1)S(1)}, bf16[5,128,256]{1,2,0:T(8,128)(2,1)S(1)}, u32[]{:S(2)}, u32[]{:S(2)}) collective-permute-start(bf16[5,128,256]{1,2,0:T(8,128)(2,1)S(1)} %pad_maximum_fusion.6), channel_id=1, source_target_pairs={{0,8},{8,16},{16,24},{24,32},{32,40},{40,48},{48,56},{56,64},{64,7... | collective-permute-start | bytes 983048 | tf_op jit(solution)/shard_map/ppermute | solution.py:14
  125.5 10.5 %collective-permute-start.4 = (bf16[5,128,256]{1,2,0:T(8,128)(2,1)S(1)}, bf16[5,128,256]{1,2,0:T(8,128)(2,1)S(1)}, u32[]{:S(2)}, u32[]{:S(2)}) collective-permute-start(bf16[5,128,256]{1,2,0:T(8,128)(2,1)S(1)} %pad_maximum_fusion.5), channel_id=1, source_target_pairs={{8,0},{16,8},{24,16},{32,24},{40,32},{48,40},{56,48},{64,56},{72,6... | collective-permute-start | bytes 983048 | tf_op jit(solution)/shard_map/ppermute | solution.py:14
  127.6 62.5 %collective-permute-start.1 = (bf16[5,128,640]{1,2,0:T(8,128)(2,1)S(1)}, bf16[5,128,640]{1,2,0:T(8,128)(2,1)S(1)}, u32[]{:S(2)}, u32[]{:S(2)}) collective-permute-start(bf16[5,128,640]{1,2,0:T(8,128)(2,1)S(1)} %get-tuple-element.115), channel_id=1, source_target_pairs={{0,8},{8,16},{16,24},{24,32},{32,40},{40,48},{48,56},{56,64},{64,7... | collective-permute-start | bytes 2457608 | tf_op jit(solution)/shard_map/ppermute | solution.py:14
  132.7 57.0 %collective-permute-start = (bf16[5,128,640]{1,2,0:T(8,128)(2,1)S(1)}, bf16[5,128,640]{1,2,0:T(8,128)(2,1)S(1)}, u32[]{:S(2)}, u32[]{:S(2)}) collective-permute-start(bf16[5,128,640]{1,2,0:T(8,128)(2,1)S(1)} %get-tuple-element.116), channel_id=1, source_target_pairs={{8,0},{16,8},{24,16},{32,24},{40,32},{48,40},{56,48},{64,56},{72,6... | collective-permute-start | bytes 2457608 | tf_op jit(solution)/shard_map/ppermute | solution.py:14
  134.6 55.8 %collective-permute-start.2 = (bf16[5,640,128]{1,2,0:T(8,128)(2,1)S(1)}, bf16[5,640,128]{1,2,0:T(8,128)(2,1)S(1)}, u32[]{:S(2)}, u32[]{:S(2)}) collective-permute-start(bf16[5,640,128]{1,2,0:T(8,128)(2,1)S(1)} %get-tuple-element.114), channel_id=1, source_target_pairs={{1,0},{2,1},{3,2},{4,3},{5,4},{6,5},{7,6},{9,8},{10,9},{11,10},{12... | collective-permute-start | bytes 2457608 | tf_op jit(solution)/shard_map/ppermute | solution.py:14
  136.1 50.0 %collective-permute-start.6 = (bf16[5,256,128]{1,2,0:T(8,128)(2,1)S(1)}, bf16[5,256,128]{1,2,0:T(8,128)(2,1)S(1)}, u32[]{:S(2)}, u32[]{:S(2)}) collective-permute-start(bf16[5,256,128]{1,2,0:T(8,128)(2,1)S(1)} %pad_maximum_fusion.7), channel_id=1, source_target_pairs={{1,0},{2,1},{3,2},{4,3},{5,4},{6,5},{7,6},{9,8},{10,9},{11,10},{12... | collective-permute-start | bytes 983048 | tf_op jit(solution)/shard_map/ppermute | solution.py:14
  137.4 52.3 %collective-permute-start.7 = (bf16[5,256,128]{1,2,0:T(8,128)(2,1)S(1)}, bf16[5,256,128]{1,2,0:T(8,128)(2,1)S(1)}, u32[]{:S(2)}, u32[]{:S(2)}) collective-permute-start(bf16[5,256,128]{1,2,0:T(8,128)(2,1)S(1)} %pad_maximum_fusion.8), channel_id=1, source_target_pairs={{0,1},{1,2},{2,3},{3,4},{4,5},{5,6},{6,7},{8,9},{9,10},{10,11},{11... | collective-permute-start | bytes 983048 | tf_op jit(solution)/shard_map/ppermute | solution.py:14
  186.0 12.6 %collective-permute-start.3 = (bf16[5,640,128]{1,2,0:T(8,128)(2,1)S(1)}, bf16[5,640,128]{1,2,0:T(8,128)(2,1)S(1)}, u32[]{:S(2)}, u32[]{:S(2)}) collective-permute-start(bf16[5,640,128]{1,2,0:T(8,128)(2,1)S(1)} %get-tuple-element.113), channel_id=1, source_target_pairs={{0,1},{1,2},{2,3},{3,4},{4,5},{5,6},{6,7},{8,9},{9,10},{10,11},{11... | collective-permute-start | bytes 2457608 | tf_op jit(solution)/shard_map/ppermute | solution.py:14
  199.1 3.2 copy-start
  199.1 14.7 %copy-start.1 = (f32[1,1,5]{2,1,0:T(1,128)S(1)}, f32[1,1,5]{2,1,0:T(1,128)}, u32[]{:S(2)}) copy-start(f32[1,1,5]{2,1,0:T(1,128)} %param.26) | copy-start | bytes 64
  221.4 26.7 %collective-permute-start.8 = (bf16[5,128,640]{1,2,0:T(8,128)(2,1)S(1)}, bf16[5,128,640]{1,2,0:T(8,128)(2,1)S(1)}, u32[]{:S(2)}, u32[]{:S(2)}) collective-permute-start(bf16[5,128,640]{1,2,0:T(8,128)(2,1)S(1)} %get-tuple-element.119), channel_id=1, source_target_pairs={{0,8},{8,16},{16,24},{24,32},{32,40},{40,48},{48,56},{56,64},{64,7... | collective-permute-start | bytes 2457608 | tf_op jit(solution)/shard_map/ppermute | solution.py:25
  223.4 24.8 %collective-permute-start.9 = (bf16[5,128,640]{1,2,0:T(8,128)(2,1)S(1)}, bf16[5,128,640]{1,2,0:T(8,128)(2,1)S(1)}, u32[]{:S(2)}, u32[]{:S(2)}) collective-permute-start(bf16[5,128,640]{1,2,0:T(8,128)(2,1)S(1)} %get-tuple-element.120), channel_id=1, source_target_pairs={{8,0},{16,8},{24,16},{32,24},{40,32},{48,40},{56,48},{64,56},{72,6... | collective-permute-start | bytes 2457608 | tf_op jit(solution)/shard_map/ppermute | solution.py:27
  248.5 17.5 %collective-permute-start.10 = (bf16[5,896,128]{1,2,0:T(8,128)(2,1)S(1)}, bf16[5,896,128]{1,2,0:T(8,128)(2,1)S(1)}, u32[]{:S(2)}, u32[]{:S(2)}) collective-permute-start(bf16[5,896,128]{1,2,0:T(8,128)(2,1)S(1)} %get-tuple-element.117), channel_id=1, source_target_pairs={{0,1},{1,2},{2,3},{3,4},{4,5},{5,6},{6,7},{8,9},{9,10},{10,11},{11... | collective-permute-start | bytes 3440648 | tf_op jit(solution)/shard_map/ppermute | solution.py:25
  252.0 42.2 %collective-permute-start.11 = (bf16[5,896,128]{1,2,0:T(8,128)(2,1)S(1)}, bf16[5,896,128]{1,2,0:T(8,128)(2,1)S(1)}, u32[]{:S(2)}, u32[]{:S(2)}) collective-permute-start(bf16[5,896,128]{1,2,0:T(8,128)(2,1)S(1)} %get-tuple-element.118), channel_id=1, source_target_pairs={{1,0},{2,1},{3,2},{4,3},{5,4},{6,5},{7,6},{9,8},{10,9},{11,10},{12... | collective-permute-start | bytes 3440648 | tf_op jit(solution)/shard_map/ppermute | solution.py:27
  266.0 33.5 %copy-start.3 = (bf16[5,896,128]{1,2,0:T(8,128)(2,1)}, bf16[5,896,128]{1,2,0:T(8,128)(2,1)S(1)}, u32[]{:S(2)}) copy-start(bf16[5,896,128]{1,2,0:T(8,128)(2,1)S(1)} %collective-permute-done.10) | copy-start | bytes 3440644
  294.2 5.2 %copy-start.4 = (bf16[5,896,128]{1,2,0:T(8,128)(2,1)}, bf16[5,896,128]{1,2,0:T(8,128)(2,1)S(1)}, u32[]{:S(2)}) copy-start(bf16[5,896,128]{1,2,0:T(8,128)(2,1)S(1)} %collective-permute-done.11) | copy-start | bytes 3440644
